TPU v7x, 256 devices: a whole 4x4x8 slice. The times are simulated.
256 devices in a mesh: section: 4 (over x), expert: 32 (over z, y), mp: 2 (over core).
Axes of the slice: x: 4, y: 4, z: 8, core: 2. Of those that a mesh axis runs over, the one named last changes fastest.
Arguments:
- out_grad: bfloat16 [4, 4096, 4096], P('section', 'expert', 'mp'), may hold values from -6 to 6
- expert_ids: int32 [4, 4096, 2], P('section', 'expert'), may hold values from 0 to 31, all different within a row; in each aligned block of 128 rows (0 to 127, 128 to 255, ..., all dimensions but the last counted through in order) at most 16 rows name the same one
- gate_codes: int32 [4, 4096, 2], P('section', 'expert'), may hold values from 1 to 255
- up_weight: bfloat16 [4, 32, 4096, 1024], P('section', 'expert', None, 'mp'), may hold values from -0.09375 to 0.09375
- down_weight: bfloat16 [4, 32, 1024, 4096], P('section', 'expert', 'mp'), may hold values from -0.1875 to 0.1875
- pre_act: bfloat16 [4, 32, 512, 1024], P('section', 'expert', None, 'mp'), may hold values from -6 to 6
- conv_grad: bfloat16 [4, 4096, 4096], P('section', 'expert', 'mp'), may hold values from -6 to 6
- conv_input: bfloat16 [4, 4096, 4096], P('section', 'expert', 'mp'), may hold values from -0.09375 to 0.09375
- conv_weight: float32 [4, 4, 4096], P('section', None, 'mp'), may hold values from -3 to 3
- in_proj: bfloat16 [4, 4096, 4096], P('section', 'expert', 'mp'), may hold values from -0.09375 to 0.09375
Outputs:
- residual_to_previous: bfloat16 [4, 4096, 4096], P('section', 'expert', 'mp')
- kernel_grad: float32 [4, 4, 4096], P('section', None, 'mp')
Inputs may be any that keep to these rules, and one draw needn't show every extreme that they name: `expert_ids`: each token names two different experts; in every section, the tokens of one block of 128 name no expert more than 16 times, a bound that some block reaches.
All inputs are finite; a program needn't handle non-finite values.
Results may differ from a plain program's by a relative error of at most 0.0044.
Values may be sent and summed in bfloat16 or wider, within the bound.
A program may use at most 128 MiB of HBM per device.

v0:
```python
import jax
import jax.numpy as jnp
from jax import lax
from jax.sharding import PartitionSpec as P


def shifted(array, axis, by):
    size = lax.axis_size(axis)
    pairs = [(i, i + by) for i in range(size) if 0 <= i + by < size]
    return lax.ppermute(array, axis, pairs)


def silu_slope(pre_value):
    sig = jax.nn.sigmoid(pre_value)
    return sig * (1.0 + pre_value * (1.0 - sig))


def gated_rows(gates, rows, tok_rows):
    scaled = (gates[:, :, None] * rows.astype(jnp.float32)[:, None, :]).astype(jnp.bfloat16)
    return scaled.reshape(tok_rows * 2, rows.shape[1])


def fill_buffer(scaled, target, experts, capacity):
    width = scaled.shape[1]
    buffer = jnp.zeros((experts * capacity, width), jnp.bfloat16).at[target].set(scaled)
    return buffer.reshape(experts, capacity, width)


def shards(
    out_grad,
    expert_ids,
    gate_codes,
    up_weight,
    down_weight,
    pre_act,
    conv_grad,
    conv_input,
    conv_weight,
    in_proj,
):
    grad_rows = out_grad[0]
    route_ids = expert_ids[0]
    tok_rows = grad_rows.shape[0]
    experts = lax.axis_size("expert")
    capacity = pre_act.shape[2] // experts
    gates = gate_codes[0].astype(jnp.float32) / 256.0
    flat_ids = route_ids.reshape(tok_rows * 2)
    onehot = (flat_ids[:, None] == jnp.arange(experts, dtype=jnp.int32)[None, :]).astype(jnp.int32)
    before = jnp.cumsum(onehot, axis=0) - onehot
    position = jnp.sum(before * onehot, axis=1)
    target = flat_ids * capacity + position
    whole_rows = lax.all_gather(grad_rows, "mp", axis=1, tiled=True)
    buffer = fill_buffer(gated_rows(gates, whole_rows, tok_rows), target, experts, capacity)
    arrived = lax.all_to_all(buffer, "expert", split_axis=0, concat_axis=0, tiled=True)
    slot_rows = arrived.reshape(experts * capacity, whole_rows.shape[1])
    w_down = down_weight[0, 0]
    w_up = up_weight[0, 0]
    pre_slots = pre_act[0, 0].astype(jnp.float32)
    hidden = lax.dot_general(
        slot_rows, w_down, (((1,), (1,)), ((), ())), preferred_element_type=jnp.float32
    )
    pre_grad = (hidden * silu_slope(pre_slots)).astype(jnp.bfloat16)
    partial_value = lax.dot_general(
        pre_grad, w_up, (((1,), (1,)), ((), ())), preferred_element_type=jnp.float32
    )
    share = lax.psum_scatter(partial_value, "mp", scatter_dimension=1, tiled=True).astype(
        jnp.bfloat16
    )
    returned = lax.all_to_all(
        share.reshape(experts, capacity, share.shape[1]),
        "expert",
        split_axis=0,
        concat_axis=0,
        tiled=True,
    )
    picked = returned.reshape(experts * capacity, grad_rows.shape[1])[target]
    picked = picked.astype(jnp.float32).reshape(tok_rows, 2, grad_rows.shape[1])
    moe_total = grad_rows.astype(jnp.float32) + picked[:, 0, :] + picked[:, 1, :]
    grads_here = conv_grad[0]
    inputs_here = conv_input[0]
    taps = conv_weight[0]
    kernel_size = taps.shape[0]
    next_rows = shifted(grads_here[: kernel_size - 1], "expert", -1)
    prev_rows = shifted(inputs_here[tok_rows - kernel_size + 1 :], "expert", 1)
    grad_ext = jnp.concatenate([grads_here, next_rows], axis=0).astype(jnp.float32)
    input_ext = jnp.concatenate([prev_rows, inputs_here], axis=0).astype(jnp.float32)
    grad_local = grads_here.astype(jnp.float32)
    conv_result = jnp.zeros(grads_here.shape, jnp.float32)
    tap_terms = []
    for tap in range(kernel_size):
        start = kernel_size - 1 - tap
        conv_result = conv_result + taps[tap][None, :] * grad_ext[start : start + tok_rows]
        tap_terms.append(jnp.sum(grad_local * input_ext[tap : tap + tok_rows], axis=0))
    input_grad = conv_result.astype(jnp.bfloat16)
    tap_grads = lax.psum(jnp.stack(tap_terms), "expert")
    w_proj = in_proj[0]
    proj_partial = lax.dot_general(
        input_grad,
        lax.all_gather(w_proj, "expert", axis=0, tiled=True),
        (((1,), (1,)), ((), ())),
        preferred_element_type=jnp.float32,
    )
    proj_share = lax.psum_scatter(proj_partial, "mp", scatter_dimension=1, tiled=True)
    residual = (moe_total + proj_share).astype(jnp.bfloat16)
    sent_residual = shifted(residual, "section", -1)
    return (sent_residual[None], tap_grads[None])


def solution(mesh):
    in_specs = (
        P("section", "expert", "mp"),
        P("section", "expert", None),
        P("section", "expert", None),
        P("section", "expert", None, "mp"),
        P("section", "expert", "mp", None),
        P("section", "expert", None, "mp"),
        P("section", "expert", "mp"),
        P("section", "expert", "mp"),
        P("section", None, "mp"),
        P("section", "expert", "mp"),
    )
    out_specs = (P("section", "expert", "mp"), P("section", None, "mp"))
    return jax.shard_map(shards, mesh=mesh, in_specs=in_specs, out_specs=out_specs, check_vma=False)
```

profile of v0, /device:TPU:6, one launch (start us, length us, event | category | flops | bytes accessed | tf_op | source)
XLA Modules:
  0.0 510.5 jit_solution(10965666901345054638)
XLA Ops:
  8.0 0.0 all-gather.5.cloned.1.call-start
  8.0 0.7 all-gather.5.cloned.1.call-update
  8.7 0.0 reduce-scatter.3.cloned.1.call-start
  8.8 0.8 copy.13
  9.6 0.1 eq.25
  9.7 0.1 eq.29
  9.8 0.7 broadcast_multiply_fusion
  10.5 0.1 copy.12
  10.6 0.1 mul.98
  10.8 0.6 reduce-window.6
  11.4 0.2 slice_reduce_fusion
  11.6 0.7 convert_multiply_fusion.5
  12.3 0.1 copy.16
  12.4 0.1 div.13
  12.6 0.1 fusion.39
  12.7 15.3 %all-gather.5.cloned.1.call-done = bf16[1,128,4096]{2,1,0:T(8,128)(2,1)} async-done(((bf16[1,128,2048]{2,1,0:T(8,128)(2,1)}), bf16[1,128,4096]{2,1,0:T(8,128)(2,1)}) %all-gather.5.cloned.1.call-update) | async-done | bytes 1048592 | tf_op jit(solution)/shard_map/all_gather | solution.py:52
  27.9 1.4 bitcast_convert_fusion
  29.4 4.4 mul.101
  33.7 6.1 %mul.102 = f32[256,4096]{1,0:T(8,128)} reshape(f32[128,2,4096]{2,1,0:T(2,128)} %mul.101) | data formatting | bytes 8388608 | tf_op jit(solution)/shard_map/mul | solution.py:19
  39.8 7.7 %scatter_custom_fusion = bf16[512,4096]{1,0:T(8,128)(2,1)} fusion(s32[256]{0:T(256)S(1)} %bitcast.99, f32[256,4096]{1,0:T(8,128)} %mul.102, f32[256]{0:T(256)S(1)} %div.13, bf16[]{:T(256)} %constant.7.clone.1), kind=kCustom, calls=%fused_computation.9 | custom fusion | flops 2097152 | bytes 8389634 | tf_op jit(solution)/shard_map/scatter | solution.py:25
  47.5 106.0 %all_to_all.10 = bf16[32,16,4096]{2,1,0:T(8,128)(2,1)S(1)} all-to-all(bf16[32,16,4096]{2,1,0:T(8,128)(2,1)} %bitcast.85), channel_id=1, replica_groups=mesh['section'=4,'expert'=32,'mp'=2] {'expert'}, dimensions={0} | all-to-all | bytes 8388608 | tf_op jit(solution)/shard_map/all_to_all | solution.py:54
  153.6 2.5 fusion.12
  156.1 5.6 %fusion.2 = f32[512,4096]{1,0:T(8,128)} fusion(bf16[512,512]{1,0:T(8,128)(2,1)S(1)} %fusion.12, bf16[1,1,4096,512]{3,2,1,0:T(8,128)(2,1)S(1)} %copy-done), kind=kOutput, calls=%fused_computation.4 | convolution fusion | flops 2147483648 | bytes 13107200 | tf_op jit(solution)/shard_map/dot_general | solution.py:63
  161.7 0.0 reduce-scatter.3.cloned.1.call-update
  161.8 0.0 all-gather.7.cloned.1.call-start
  161.8 0.5 all-gather.7.cloned.1.call-update
  162.3 0.4 copy-done.1
  162.8 1.3 collective-permute-start
  164.1 4.3 collective-permute-done
  168.4 0.1 maximum_convert_fusion
  168.5 12.6 %reduce-scatter.3.cloned.1.call-done = f32[512,2048]{1,0:T(8,128)} async-done(((f32[512,4096]{1,0:T(8,128)}), f32[512,2048]{1,0:T(8,128)}) %reduce-scatter.3.cloned.1.call-update) | async-done | bytes 4194320 | tf_op jit(solution)/shard_map/reduce_scatter | solution.py:66
  181.2 3.9 convert_element_type.68
  185.0 9.8 %all-to-all-start.1 = ((bf16[32,16,2048]{2,1,0:T(8,128)(2,1)}), bf16[32,16,2048]{2,1,0:T(8,128)(2,1)S(1)}, u32[]{:S(2)}, u32[]{:S(2)}) async-start(bf16[32,16,2048]{2,1,0:T(8,128)(2,1)} %bitcast.86), calls=%async_computation.2 | async-start | bytes 4194304 | tf_op jit(solution)/shard_map/all_to_all | solution.py:69
  194.8 0.0 reduce-scatter.5.cloned.1.call-start
  194.9 133.4 %all-gather.7.cloned.1.call-done = bf16[1,4096,2048]{2,1,0:T(8,128)(2,1)} async-done(((bf16[1,128,2048]{2,1,0:T(8,128)(2,1)}), bf16[1,4096,2048]{2,1,0:T(8,128)(2,1)}) %all-gather.7.cloned.1.call-update) | async-done | bytes 16777232 | tf_op jit(solution)/shard_map/all_gather | solution.py:99
  328.3 12.8 %fusion = f32[128,4096]{1,0:T(8,128)} fusion(bf16[1,4096,2048]{2,1,0:T(8,128)(2,1)} %all-gather.7.cloned.1.call-done, f32[131,2048]{1,0:T(8,128)S(1)} %maximum_convert_fusion, f32[2048]{0:T(1024)S(1)} %bitcast.93, f32[2048]{0:T(1024)S(1)} %bitcast.94, f32[2048]{0:T(1024)S(1)} %bitcast.92, f32[2048]{0:T(1024)S(1)} %bitcast.91), kind=kOutput, calls=%fused_computation.2 | convolution fusion | flops 2149580800 | bytes 23101440 | tf_op jit(solution)/shard_map/dot_general | solution.py:97
  341.1 0.8 slice_bitcast_fusion
  341.9 2.1 collective-permute-start.2
  344.0 1.4 gather_fusion
  345.4 1.3 reshape.97
  346.7 2.7 fusion.41
  349.4 4.0 reduce-scatter.5.cloned.1.call-done
  353.4 2.4 fusion.30
  355.8 2.8 collective-permute-start.1
  358.7 0.1 maximum_convert_fusion.1
  358.8 0.6 fusion.20
  359.4 143.1 %psum.7 = f32[1,4,2048]{2,1,0:T(4,128)} all-reduce(f32[1,4,2048]{2,1,0:T(4,128)S(1)} %maximum_bitcast_fusion), channel_id=1, replica_groups=mesh['section'=4,'expert'=32,'mp'=2] {'expert'}, use_global_device_ids=true, to_apply=%region_10.11 | all-reduce | flops 8192 | bytes 65536 | tf_op jit(solution)/shard_map/psum | solution.py:95
  502.6 0.8 copy.36
  (25 shorter events, 0.2 us)
Async XLA Ops:
  8.0 19.9 %all-gather.5.cloned.1.call-start = ((), (), s32[]{:S(2)}) async-start(), calls=%async_computation.6 | async-start | bytes 1572864 | tf_op jit(solution)/shard_map/all_gather | solution.py:52
  8.7 172.4 %reduce-scatter.3.cloned.1.call-start = ((), (), s32[]{:S(2)}) async-start(), calls=%async_computation.4 | async-start | bytes 12582912 | tf_op jit(solution)/shard_map/reduce_scatter | solution.py:66
  47.5 106.0 %copy-start.5 = (bf16[1,1,512,4096]{3,2,1,0:T(8,128)(2,1)S(1)}, bf16[1,1,512,4096]{3,2,1,0:T(8,128)(2,1)}, u32[]{:S(2)}) copy-start(bf16[1,1,512,4096]{3,2,1,0:T(8,128)(2,1)} %param.14) | copy-start | bytes 12582916
  47.5 106.0 %copy-start.6 = (bf16[1,1,512,512]{3,2,1,0:T(8,128)(2,1)S(1)}, bf16[1,1,512,512]{3,2,1,0:T(8,128)(2,1)}, u32[]{:S(2)}) copy-start(bf16[1,1,512,512]{3,2,1,0:T(8,128)(2,1)} %param.15) | copy-start | bytes 1572868
  153.6 2.6 copy-start
  161.7 1.0 copy-start.1
  161.7 2.4 copy-start.4
  161.8 166.5 %all-gather.7.cloned.1.call-start = ((), (), s32[]{:S(2)}) async-start(), calls=%async_computation.7 | async-start | bytes 17301504 | tf_op jit(solution)/shard_map/all_gather | solution.py:99
  162.8 5.6 %collective-permute-start = (bf16[3,2048]{1,0:T(4,128)(2,1)S(1)}, bf16[3,2048]{1,0:T(4,128)(2,1)S(1)}, u32[]{:S(2)}, u32[]{:S(2)}) collective-permute-start(bf16[3,2048]{1,0:T(4,128)(2,1)S(1)} %slice_bitcast_fusion.1), channel_id=1, source_target_pairs={{2,0},{4,2},{6,4},{8,6},{10,8},{12,10},{14,12},{16,14},{18,16},{20... | collective-permute-start | bytes 36872 | tf_op jit(solution)/shard_map/ppermute | solution.py:10
  185.0 159.0 %all-to-all-start.1 = ((bf16[32,16,2048]{2,1,0:T(8,128)(2,1)}), bf16[32,16,2048]{2,1,0:T(8,128)(2,1)S(1)}, u32[]{:S(2)}, u32[]{:S(2)}) async-start(bf16[32,16,2048]{2,1,0:T(8,128)(2,1)} %bitcast.86), calls=%async_computation.2 | async-start | bytes 4194304 | tf_op jit(solution)/shard_map/all_to_all | solution.py:69
  194.8 158.6 %reduce-scatter.5.cloned.1.call-start = ((), (), s32[]{:S(2)}) async-start(), calls=%async_computation.5 | async-start | bytes 3145728 | tf_op jit(solution)/shard_map/reduce_scatter | solution.py:103
  341.9 16.7 %collective-permute-start.2 = (bf16[3,2048]{1,0:T(4,128)(2,1)S(1)}, bf16[3,2048]{1,0:T(4,128)(2,1)S(1)}, u32[]{:S(2)}, u32[]{:S(2)}) collective-permute-start(bf16[3,2048]{1,0:T(4,128)(2,1)S(1)} %slice_bitcast_fusion), channel_id=1, source_target_pairs={{0,2},{2,4},{4,6},{6,8},{8,10},{10,12},{12,14},{14,16},{16,18},{18... | collective-permute-start | bytes 36872 | tf_op jit(solution)/shard_map/ppermute | solution.py:10
  349.4 9.3 %copy-start.3 = (bf16[1,128,2048]{2,1,0:T(8,128)(2,1)S(1)}, bf16[1,128,2048]{2,1,0:T(8,128)(2,1)}, u32[]{:S(2)}) copy-start(bf16[1,128,2048]{2,1,0:T(8,128)(2,1)} %param.17) | copy-start | bytes 1572868
  349.4 9.4 %copy-start.2 = (bf16[1,128,2048]{2,1,0:T(8,128)(2,1)S(1)}, bf16[1,128,2048]{2,1,0:T(8,128)(2,1)}, u32[]{:S(2)}) copy-start(bf16[1,128,2048]{2,1,0:T(8,128)(2,1)} %param.16) | copy-start | bytes 1572868
  355.8 146.7 %collective-permute-start.1 = (bf16[128,2048]{1,0:T(8,128)(2,1)S(1)}, bf16[128,2048]{1,0:T(8,128)(2,1)S(1)}, u32[]{:S(2)}, u32[]{:S(2)}) collective-permute-start(bf16[128,2048]{1,0:T(8,128)(2,1)S(1)} %fusion.30), channel_id=1, source_target_pairs={{64,0},{128,64},{192,128},{65,1},{129,65},{193,129},{66,2},{130,66... | collective-permute-start | bytes 1572872 | tf_op jit(solution)/shard_map/ppermute | solution.py:10
Sparse Core Ops, SparseCore 0:
  10.6 17.2 all-gather.4
  161.9 19.2 reduce-scatter.2
  341.3 12.0 reduce-scatter.4
Sparse Core Ops, SparseCore 1:
  165.1 163.1 all-gather.6
where the time goes:
time: 511 us; the launch traced here: 510 us
  blocking collectives  249 us (49%)
  waiting for transfers between devices  171 us (33%)
  matrix products  21 us (4%)
  local copies, waits for them, and re-layouts  19.6 us (4%)
  other arithmetic  18.5 us (4%)
  starting transfers between devices  16.1 us (3%)
  between operations  15.4 us (3%)
    psum x1, blocking collectives, shards(): tap_grads = lax.psum(jnp.stack(tap_terms), 'expert')  143 us
    all_gather x1, waiting for transfers between devices, shards(): lax.all_gather(w_proj, 'expert', axis=0, tiled=True)  133 us
    all_to_all x1, blocking collectives, shards(): lax.all_to_all(buffer, 'expert', split_axis=0, concat_axis=0, tiled=True)  106 us
    all_gather x1, waiting for transfers between devices, shards(): whole_rows = lax.all_gather(grad_rows, 'mp', axis=1, tiled=True)  15.3 us
    dot_general x1, matrix products, shards(): lax.dot_general(input_grad, lax.all_gather(w_proj, 'expert', axis=0, tile...  12.8 us
    reduce_scatter x1, waiting for transfers between devices, shards(): lax.psum_scatter(partial_value, 'mp', scatter_dimension=1, tiled=True)  12.6 us
    mul x2, local copies, waits for them, and re-layouts, gated_rows(): gates[:, :, None] * rows.astype(jnp.float32)[:, None, :]  10.4 us
  transfers between devices with their start and end apart: 8, of which 5 were waited for; matrix products, arithmetic and copies ran while one was open for 6% of the time, Pallas kernels for 0%

commit v1 on v0

v1 whole, which is shorter than its diff:
```python
import jax
import jax.numpy as jnp
from jax import lax
from jax.experimental import pallas as pl
from jax.experimental.pallas import tpu as pltpu
from jax.sharding import PartitionSpec as P

MESH = pl.DeviceIdType.MESH
F32 = jnp.float32
BF16 = jnp.bfloat16

NY = 4
NZ = 8
CAP = 16
TOK = 128
HALF = 2048
NSEC = 4
NEXP = 32
NT = (((1,), (1,)), ((), ()))


def dot_nt(a, b):
    return lax.dot_general(a, b, NT, preferred_element_type=F32)


def silu_slope(pre_value):
    sig = 1.0 / (1.0 + jnp.exp(-pre_value))
    return sig * (1.0 + pre_value * (1.0 - sig))


def kernel(
    og, ids, codes, cg, ci, cw, bp, up, down, pre,
    out, kout,
    wdn, wup, prev_, sbuf, xin, yout, ret, comb, comb_r, og_r,
    bg, ag, halo_g, halo_i, gext, iext, part, part_r, psend, prec,
    tap_p, tap_r, tap_s, tap_z, tap_t, tap_o,
    lsem, wsend, wrecv, hsend, hrecv, osend, orecv,
    bsend, brecv, xsend, xrecv, ysend, yrecv, asend, arecv,
    psem_s, psem_r, qsend, qrecv, tsend, trecv,
):
    sec = lax.axis_index("section")
    me = lax.axis_index("expert")
    core = lax.axis_index("mp")
    z = me // NY
    y = me % NY
    mine = z // 4
    other = 1 - core
    partner = (sec, me, other)

    def rcopy(src, dst, ssem, rsem, dev):
        return pltpu.make_async_remote_copy(
            src_ref=src, dst_ref=dst, send_sem=ssem, recv_sem=rsem,
            device_id=dev, device_id_type=MESH,
        )

    def wait_in(dst, rsem):
        rcopy(dst, dst, lsem.at[0], rsem, partner).wait_recv()

    def wait_out(src, ssem):
        rcopy(src, src, ssem, lsem.at[0], partner).wait_send()

    def zdev(dz):
        return (sec, ((z + dz + NZ) % NZ) * NY + y, core)

    def ydev(dy):
        return (sec, z * NY + (y + dy) % NY, core)

    def rows(start, size):
        return pl.ds(pl.multiple_of(start, size), size)

    has_next = me < NEXP - 1
    has_prev = me > 0
    halo_g_out = rcopy(cg.at[pl.ds(0, 16)], halo_g, hsend.at[0], hrecv.at[0], (sec, me - 1, core))
    halo_i_out = rcopy(ci.at[pl.ds(TOK - 16, 16)], halo_i, hsend.at[1], hrecv.at[1], (sec, me + 1, core))

    @pl.when(has_prev)
    def _():
        halo_g_out.start()

    @pl.when(has_next)
    def _():
        halo_i_out.start()

    def ring(step, up_way):
        shard = (z - (step - 1) + NZ) % NZ if up_way else (z + (step - 1)) % NZ
        way = 0 if up_way else 1
        start, size = (0, TOK) if step < 4 else ((0, 64) if up_way else (64, 64))
        block = pl.ds(pl.multiple_of(shard * TOK + start, 64), size)
        src = bp if step == 1 else bg.at[block]
        return rcopy(src, bg.at[block], bsend.at[step - 1, way], brecv.at[step - 1, way], zdev(1 if up_way else -1))

    def ring_arrived(step):
        for way in range(2):
            shard = (z - step + NZ) % NZ if way == 0 else (z + step) % NZ
            start, size = (0, TOK) if step < 4 else ((0, 64) if way == 0 else (64, 64))
            block = pl.ds(pl.multiple_of(shard * TOK + start, 64), size)
            wait_in(bg.at[block], brecv.at[step - 1, way])

    def ring_go(step):
        if step > 1:
            ring_arrived(step - 1)
        ring(step, True).start()
        ring(step, False).start()

    own_rows = pltpu.make_async_copy(bp, bg.at[rows(z * TOK, TOK)], lsem.at[4])
    own_down = pltpu.make_async_copy(down, wdn.at[core], lsem.at[1])
    own_up = pltpu.make_async_copy(up, wup.at[core], lsem.at[2])
    own_pre = pltpu.make_async_copy(pre.at[rows(core * 256, 256)], prev_.at[core], lsem.at[3])
    give_down = rcopy(down, wdn.at[core], wsend.at[0], wrecv.at[0], partner)
    give_up = rcopy(up, wup.at[core], wsend.at[1], wrecv.at[1], partner)
    give_pre = rcopy(pre.at[rows(other * 256, 256)], prev_.at[core], wsend.at[2], wrecv.at[2], partner)
    give_og = rcopy(og, og_r, osend.at[0], orecv.at[0], (sec - 1, me, core))
    give_comb = rcopy(comb, comb_r, osend.at[1], orecv.at[1], (sec - 1, me, core))

    active = sec > 0

    def block_copy(e):
        return rcopy(
            sbuf.at[rows(e * CAP, CAP)],
            xin.at[core, rows((me % 16) * CAP, CAP)],
            xsend.at[e], xrecv.at[me % 16, core], (sec, e, mine),
        )

    def block_local(e):
        return pltpu.make_async_copy(
            sbuf.at[rows(e * CAP, CAP)],
            xin.at[core, rows((me % 16) * CAP, CAP)],
            xrecv.at[me % 16, core],
        )

    @pl.when(active)
    def _():
        ring_go(1)
        own_rows.start()

        lane = lax.broadcasted_iota(jnp.int32, (TOK, NEXP * CAP), 1)
        expert = lane // CAP
        rank = lane % CAP
        first = ids[:, 0:1] == expert
        second = ids[:, 1:2] == expert
        named = first | second
        gates = codes[...].astype(F32) / 256.0
        gate = jnp.where(first, gates[:, 0:1], 0.0) + jnp.where(second, gates[:, 1:2], 0.0)
        low = lax.broadcasted_iota(jnp.int32, (TOK, TOK), 1) < lax.broadcasted_iota(jnp.int32, (TOK, TOK), 0)
        before = jnp.dot(
            jnp.where(low, 1.0, 0.0).astype(BF16),
            jnp.where(named, 1.0, 0.0).astype(BF16),
            preferred_element_type=F32,
        )
        here = named & (before == rank.astype(F32))
        comb[...] = jnp.where(here, 1.0, 0.0).astype(BF16)
        placed = jnp.where(here, gate, 0.0).T.astype(BF16)
        for tile in range(4):
            cols = pl.ds(tile * 512, 512)
            sbuf[:, cols] = jnp.dot(placed, og[:, cols], preferred_element_type=F32).astype(BF16)

        def send_block(i, carry):
            turn = i // 8
            zt = (z - turn + 8) % 4 + 4 * ((i // 4) % 2)
            e = zt * NY + (y + i) % NY
            own = (e == me) & (mine == core)

            @pl.when(own)
            def _():
                block_local(e).start()

            @pl.when(jnp.logical_not(own))
            def _():
                block_copy(e).start()

            return carry

        lax.fori_loop(0, NEXP, send_block, 0)
        own_down.start()
        own_up.start()
        own_pre.start()
        give_down.start()
        give_pre.start()
        give_up.start()
        give_og.start()
        give_comb.start()

    @pl.when(has_next)
    def _():
        wait_in(halo_g, hrecv.at[0])

    @pl.when(jnp.logical_not(has_next))
    def _():
        halo_g[...] = jnp.zeros_like(halo_g)

    @pl.when(has_prev)
    def _():
        wait_in(halo_i, hrecv.at[1])

    @pl.when(jnp.logical_not(has_prev))
    def _():
        halo_i[...] = jnp.zeros_like(halo_i)

    gext[pl.ds(0, TOK), :] = cg[...].astype(F32)
    gext[pl.ds(TOK, 8), :] = halo_g[...].astype(F32)[0:8]
    iext[pl.ds(0, 8), :] = halo_i[...].astype(F32)[8:16]
    iext[pl.ds(8, TOK), :] = ci[...].astype(F32)
    tap_p[...] = jnp.zeros_like(tap_p)

    for quarter in range(4):
        @pl.loop(0, 4)
        def _(i):
            cols = pl.ds(pl.multiple_of(quarter * 512 + i * 128, 128), 128)
            lanes = pl.ds(pl.multiple_of(i * 128, 128), 128)
            grad = gext[pl.ds(0, TOK), cols]
            total = jnp.zeros((TOK, 128), F32)
            for tap in range(4):
                total = total + cw[tap : tap + 1, cols] * gext[pl.ds(3 - tap, TOK), cols]
                term = grad * iext[pl.ds(5 + tap, TOK), cols]
                tap_p[quarter, tap : tap + 1, lanes] = jnp.sum(term, axis=0, keepdims=True)
            ag[rows(y * TOK, TOK), cols] = total.astype(BF16)

    def tap_scatter(dy):
        to = (y + dy) % NY
        return rcopy(tap_p.at[to], tap_r.at[y], tsend.at[0, dy - 1], trecv.at[0, y], ydev(dy))

    for dy in range(1, NY):
        tap_scatter(dy).start()

    def a_copy(dy):
        block = rows(y * TOK, TOK)
        return rcopy(ag.at[block], ag.at[block], asend.at[dy - 1], arecv.at[y], ydev(dy))

    @pl.when(active)
    def _():
        for dy in range(1, NY):
            a_copy(dy).start()
        ring_go(2)

    tap_r[y] = tap_p[y]
    for dy in range(1, NY):
        wait_in(tap_r.at[(y + dy) % NY], trecv.at[0, (y + dy) % NY])
    tap_s[...] = (tap_r[0] + tap_r[1]) + (tap_r[2] + tap_r[3])

    def tap_gather(dz):
        return rcopy(tap_s, tap_z.at[z], tsend.at[1, dz - 1], trecv.at[1, z], zdev(dz))

    for dz in range(1, NZ):
        tap_gather(dz).start()

    def back(src, half):
        return rcopy(
            yout.at[half, rows(src * CAP, CAP)],
            ret.at[rows(me * CAP, CAP)],
            ysend.at[src, half], yrecv.at[me],
            (sec - 1, core * 16 + src, half),
        )

    def expert_chunk(turn):
        zs = (turn + z) % 4
        block = rows(zs * 64, 64)

        def arrive(i, carry):
            src = zs * NY + i // 2
            wait_in(xin.at[i % 2, rows(src * CAP, CAP)], xrecv.at[src, i % 2])
            return carry

        lax.fori_loop(0, 8, arrive, 0)
        if turn == 0:
            own_down.wait()
            wait_in(wdn.at[other], wrecv.at[0])
            own_pre.wait()
            wait_in(prev_.at[other], wrecv.at[2])
        x0 = xin[0, block, :]
        x1 = xin[1, block, :]
        grads = []
        for h in range(2):
            hidden = dot_nt(x0, wdn[h, :, 0:HALF]) + dot_nt(x1, wdn[h, :, HALF:])
            slope = silu_slope(prev_[h, block, :].astype(F32))
            grads.append((hidden * slope).astype(BF16))
        if turn == 0:
            own_up.wait()
            wait_in(wup.at[other], wrecv.at[1])
        for half in range(2):
            @pl.loop(0, 4)
            def _(t):
                wide = pl.ds(pl.multiple_of(half * HALF + t * 512, 512), 512)
                cols = pl.ds(pl.multiple_of(t * 512, 512), 512)
                value = dot_nt(grads[0], wup[0, wide, :]) + dot_nt(grads[1], wup[1, wide, :])
                yout[half, block, cols] = value.astype(BF16)

        def give(i, carry):
            back(zs * NY + (y + i // 2) % NY, i % 2).start()
            return carry

        lax.fori_loop(0, 8, give, 0)

    @pl.when(active)
    def _():
        expert_chunk(0)
        ring_go(3)
        expert_chunk(1)
        ring_go(4)
        expert_chunk(2)

    tap_z[z] = tap_s[...]
    for dz in range(1, NZ):
        wait_in(tap_z.at[(z + dz) % NZ], trecv.at[1, (z + dz) % NZ])
    total = tap_z[0]
    for i in range(1, NZ):
        total = total + tap_z[i]
    tap_t[...] = total

    def tap_share(dy):
        return rcopy(tap_t, tap_o.at[y], tsend.at[2, dy - 1], trecv.at[2, y], ydev(dy))

    for dy in range(1, NY):
        tap_share(dy).start()

    give_part = rcopy(part.at[other], part_r, psem_s.at[0], psem_r.at[0], partner)

    def proj_back(to):
        return rcopy(psend.at[to], prec.at[y], qsend.at[to], qrecv.at[y], (sec - 1, z * NY + to, core))

    @pl.when(active)
    def _():
        expert_chunk(3)
        for dy in range(1, NY):
            wait_in(ag.at[rows(((y + dy) % NY) * TOK, TOK)], arecv.at[(y + dy) % NY])
        ring_arrived(4)
        own_rows.wait()

        def product(h):
            @pl.loop(0, 4)
            def _(i):
                tokens = pl.ds(pl.multiple_of((i // 2) * 256, 256), 256)
                cols = pl.ds(pl.multiple_of((i % 2) * 256, 256), 256)
                wide = pl.ds(pl.multiple_of(h * 512 + (i % 2) * 256, 256), 256)
                part[h, tokens, cols] = dot_nt(ag[tokens, :], bg[wide, :])

        product(other)
        give_part.start()
        product(core)
        wait_in(part_r, psem_r.at[0])
        for to in range(NY):
            tokens = pl.ds(to * TOK, TOK)
            psend[to] = (part[core, tokens, :] + part_r[tokens, :]).astype(BF16)
        for to in range(NY):
            proj_back(to).start()

    @pl.when(sec < NSEC - 1)
    def _():
        wait_in(og_r, orecv.at[0])
        wait_in(comb_r, orecv.at[1])
        for i in range(NY):
            wait_in(prec.at[i], qrecv.at[i])

        def arrive(i, carry):
            wait_in(ret.at[rows(i * CAP, CAP)], yrecv.at[i])
            return carry

        lax.fori_loop(0, NEXP, arrive, 0)
        for tile in range(4):
            cols = pl.ds(tile * 512, 512)
            proj = jnp.concatenate([prec[i, :, tile * 128 : tile * 128 + 128] for i in range(NY)], axis=1)
            moe = jnp.dot(comb_r[...], ret[:, cols], preferred_element_type=F32)
            out[:, cols] = (og_r[:, cols].astype(F32) + moe + proj.astype(F32)).astype(BF16)

    @pl.when(sec == NSEC - 1)
    def _():
        out[...] = jnp.zeros_like(out)

    tap_o[y] = tap_t[...]
    for dy in range(1, NY):
        wait_in(tap_o.at[(y + dy) % NY], trecv.at[2, (y + dy) % NY])
    for quarter in range(4):
        kout[:, pl.ds(quarter * 512, 512)] = tap_o[quarter, 0:4, :]

    @pl.when(has_prev)
    def _():
        halo_g_out.wait_send()

    @pl.when(has_next)
    def _():
        halo_i_out.wait_send()

    for dy in range(1, NY):
        tap_scatter(dy).wait_send()
        tap_share(dy).wait_send()
    for dz in range(1, NZ):
        tap_gather(dz).wait_send()

    @pl.when(active)
    def _():
        for step in range(1, 5):
            ring(step, True).wait_send()
            ring(step, False).wait_send()
        for dy in range(1, NY):
            a_copy(dy).wait_send()
        give_down.wait_send()
        give_up.wait_send()
        give_pre.wait_send()
        give_og.wait_send()
        give_comb.wait_send()
        give_part.wait_send()
        for to in range(NY):
            proj_back(to).wait_send()

        def sent(e, carry):
            own = (e == me) & (mine == core)

            @pl.when(jnp.logical_not(own))
            def _():
                block_copy(e).wait_send()

            back(e // 2, e % 2).wait_send()
            return carry

        lax.fori_loop(0, NEXP, sent, 0)


def shards(
    out_grad, expert_ids, gate_codes, up_weight, down_weight, pre_act, conv_grad, conv_input, conv_weight, in_proj
):
    vmem = pl.BlockSpec(memory_space=pltpu.VMEM)
    anywhere = pl.BlockSpec(memory_space=pl.ANY)
    dma = pltpu.SemaphoreType.DMA
    out, kout = pl.pallas_call(
        kernel,
        out_shape=(
            jax.ShapeDtypeStruct((TOK, HALF), BF16),
            jax.ShapeDtypeStruct((4, HALF), F32),
        ),
        in_specs=[vmem] * 7 + [anywhere] * 3,
        out_specs=(vmem, vmem),
        scratch_shapes=[
            pltpu.VMEM((2, 512, 4096), BF16),
            pltpu.VMEM((2, 4096, 512), BF16),
            pltpu.VMEM((2, 256, 512), BF16),
            pltpu.VMEM((512, HALF), BF16),
            pltpu.VMEM((2, 256, HALF), BF16),
            pltpu.VMEM((2, 256, HALF), BF16),
            pltpu.VMEM((512, HALF), BF16),
            pltpu.VMEM((TOK, 512), BF16),
            pltpu.VMEM((TOK, 512), BF16),
            pltpu.VMEM((TOK, HALF), BF16),
            pltpu.VMEM((NZ * TOK, HALF), BF16),
            pltpu.VMEM((NY * TOK, HALF), BF16),
            pltpu.VMEM((16, HALF), BF16),
            pltpu.VMEM((16, HALF), BF16),
            pltpu.VMEM((TOK + 8, HALF), F32),
            pltpu.VMEM((TOK + 8, HALF), F32),
            pltpu.VMEM((2, 512, 512), F32),
            pltpu.VMEM((512, 512), F32),
            pltpu.VMEM((NY, TOK, 512), BF16),
            pltpu.VMEM((NY, TOK, 512), BF16),
            pltpu.VMEM((NY, 8, 512), F32),
            pltpu.VMEM((NY, 8, 512), F32),
            pltpu.VMEM((8, 512), F32),
            pltpu.VMEM((NZ, 8, 512), F32),
            pltpu.VMEM((8, 512), F32),
            pltpu.VMEM((NY, 8, 512), F32),
            dma((5,)),
            dma((3,)), dma((3,)),
            dma((2,)), dma((2,)),
            dma((2,)), dma((2,)),
            dma((4, 2)), dma((4, 2)),
            dma((NEXP,)), dma((16, 2)),
            dma((16, 2)), dma((NEXP,)),
            dma((3,)), dma((NY,)),
            dma((1,)), dma((1,)),
            dma((NY,)), dma((NY,)),
            dma((3, 7)), dma((3, NZ)),
        ],
        compiler_params=pltpu.CompilerParams(has_side_effects=True, vmem_limit_bytes=60 * 1024 * 1024),
        name="layer_backward",
    )(
        out_grad[0], expert_ids[0], gate_codes[0], conv_grad[0], conv_input[0], conv_weight[0], in_proj[0],
        up_weight[0, 0], down_weight[0, 0], pre_act[0, 0],
    )
    return out[None], kout[None]


def solution(mesh):
    in_specs = (
        P("section", "expert", "mp"),
        P("section", "expert", None),
        P("section", "expert", None),
        P("section", "expert", None, "mp"),
        P("section", "expert", "mp", None),
        P("section", "expert", None, "mp"),
        P("section", "expert", "mp"),
        P("section", "expert", "mp"),
        P("section", None, "mp"),
        P("section", "expert", "mp"),
    )
    out_specs = (P("section", "expert", "mp"), P("section", None, "mp"))
    return jax.shard_map(shards, mesh=mesh, in_specs=in_specs, out_specs=out_specs, check_vma=False)
```

time: 511 us -> 183 us (0.36)
  the two profiles are of different devices: /device:TPU:6 before, /device:TPU:37 now
where the time goes in v1:
time: 183 us; the launch traced here: 180 us
  Pallas kernels  173 us (95%)
  local copies, waits for them, and re-layouts  6.09 us (3%)
    pallas_call x1, Pallas kernels, shards(): pl.pallas_call(kernel, out_shape=(jax.ShapeDtypeStruct((TOK, HALF), BF16)...  173 us
    unnamed x4, local copies, waits for them, and re-layouts  6.09 us

profile of v1, /device:TPU:37, one launch (start us, length us, event | category | flops | bytes accessed | tf_op | source)
XLA Modules:
  0.0 180.0 jit_solution(10390412883578512562)
XLA Ops:
  0.6 1.4 copy.12
  2.0 1.4 copy.13
  3.5 173.3 %layer_backward.1 = (bf16[128,2048]{1,0:T(8,128)(2,1)}, f32[4,2048]{1,0:T(4,128)}) custom-call(bf16[128,2048]{1,0:T(8,128)(2,1)} %bitcast.14, s32[128,2]{1,0:T(8,128)} %bitcast.20, s32[128,2]{1,0:T(8,128)} %bitcast.21, bf16[128,2048]{1,0:T(8,128)(2,1)} %bitcast.15, bf16[128,2048]{1,0:T(8,128)(2,1)} %bitcast.16, f32[4,2048]{1,0:T(4,128)} %bitcast.22, ...), custom_call_target="tpu_custom_call" | custom-call | tf_op jit(solution)/shard_map/layer_backward/pallas_call | solution.py:423
  176.8 1.9 %copy.16 = bf16[1,128,2048]{2,1,0:T(8,128)(2,1)} copy(bf16[1,128,2048]{2,1,0:T(8,128)(2,1)} %bitcast.19) | data formatting | bytes 1048576
  178.7 1.4 copy.17

commit v2 on v1

v2 whole, which is shorter than its diff:
```python
import jax
import jax.numpy as jnp
from jax import lax
from jax.experimental import pallas as pl
from jax.experimental.pallas import tpu as pltpu
from jax.sharding import PartitionSpec as P

MESH = pl.DeviceIdType.MESH
F32 = jnp.float32
BF16 = jnp.bfloat16

NY = 4
NZ = 8
CAP = 16
TOK = 128
HALF = 2048
NSEC = 4
NEXP = 32
SPREAD = 2
CHUNK = 2048 // SPREAD
WIDE = CHUNK + 2 * HALF
NT = (((1,), (1,)), ((), ()))


def dot_nt(a, b):
    return lax.dot_general(a, b, NT, preferred_element_type=F32)


def silu_slope(pre_value):
    sig = 1.0 / (1.0 + jnp.exp(-pre_value))
    return sig * (1.0 + pre_value * (1.0 - sig))


def kernel(
    og, ids, codes, cg, ci, cw, bp, up, down, pre,
    out, kout,
    wdn, wup, prev_, sbuf, xin, yout, ret, comb, res,
    bg, ag, gin, cwin, halo_i, gext, iext, psend, prec, base,
    tap_p, tap_r, tap_s, tap_z, tap_t, tap_o,
    lsem, wsend, wrecv, hsend, hrecv, osend, orecv,
    bsend, brecv, xsend, xrecv, ysend, yrecv, asend, arecv,
    jsend, jrecv, qsend, qrecv, tsend, trecv,
):
    sec = lax.axis_index("section")
    me = lax.axis_index("expert")
    core = lax.axis_index("mp")
    z = me // NY
    y = me % NY
    mine = z // 4
    other = 1 - core
    partner = (sec, me, other)

    def rcopy(src, dst, ssem, rsem, dev):
        return pltpu.make_async_remote_copy(
            src_ref=src, dst_ref=dst, send_sem=ssem, recv_sem=rsem,
            device_id=dev, device_id_type=MESH,
        )

    def wait_in(dst, rsem):
        rcopy(dst, dst, lsem.at[0], rsem, partner).wait_recv()

    def wait_out(src, ssem):
        rcopy(src, src, ssem, lsem.at[0], partner).wait_send()

    def zdev(dz):
        return (sec, ((z + dz + NZ) % NZ) * NY + y, core)

    def ydev(dy):
        return (sec, z * NY + (y + dy) % NY, core)

    def rows(start, size):
        return pl.ds(pl.multiple_of(start, size), size)

    has_next = me < NEXP - 1
    has_prev = me > 0
    active = sec > 0
    fed = sec < NSEC - 1

    barrier = pltpu.get_barrier_semaphore()

    def greet(i, carry):
        pl.semaphore_signal(
            barrier, inc=1, device_id=(sec, (me + i // 2) % NEXP, (core + i) % 2), device_id_type=MESH
        )
        return carry

    lax.fori_loop(1, 2 * NEXP, greet, 0)

    def greet_far(i, carry):
        there = ((sec + 1 + i // 8) % NSEC, z * NY + (i // 2) % NY, i % 2)
        pl.semaphore_signal(barrier, inc=1, device_id=there, device_id_type=MESH)
        return carry

    lax.fori_loop(0, 24, greet_far, 0)

    def greet_side(i, carry):
        side = me + 2 * (i % 2) - 1

        @pl.when((side >= 0) & (side < NEXP))
        def _():
            there = ((sec + 1 + i // 4) % NSEC, side, (i // 2) % 2)
            pl.semaphore_signal(barrier, inc=1, device_id=there, device_id_type=MESH)

        return carry

    lax.fori_loop(0, 12, greet_side, 0)

    halo_i_out = rcopy(ci.at[pl.ds(TOK - 16, 16)], halo_i, hsend.at[1], hrecv.at[1], (sec, me + 1, core))

    JOBS = ((2, 0, CHUNK), (1, CHUNK, HALF), (3, CHUNK + HALF, HALF))
    runs = sec >= NSEC - SPREAD

    def job_cols(job):
        return pl.ds(JOBS[job][1], JOBS[job][2])

    def ring(job, step, up_way):
        shard = (z - (step - 1) + NZ) % NZ if up_way else (z + (step - 1)) % NZ
        way = 0 if up_way else 1
        start, size = (0, TOK) if step < 4 else ((0, 64) if up_way else (64, 64))
        block = bg.at[pl.ds(pl.multiple_of(shard * TOK + start, 64), size), job_cols(job)]
        return rcopy(
            block, block, bsend.at[job, step - 1, way], brecv.at[job, step - 1, way], zdev(1 if up_way else -1)
        )

    def ring_arrived(job, step):
        for way in range(2):
            shard = (z - step + NZ) % NZ if way == 0 else (z + step) % NZ
            start, size = (0, TOK) if step < 4 else ((0, 64) if way == 0 else (64, 64))
            block = pl.ds(pl.multiple_of(shard * TOK + start, 64), size)
            wait_in(bg.at[block, job_cols(job)], brecv.at[job, step - 1, way])

    def ring_go(job, step):
        if step == 1:
            wait_in(bg.at[rows(z * TOK, TOK), job_cols(job)], jrecv.at[job, 0])
        else:
            ring_arrived(job, step - 1)
        ring(job, step, True).start()
        ring(job, step, False).start()

    def slice_of(i):
        piece = core * SPREAD + i
        return pl.ds(i * CHUNK, CHUNK), 3 - piece // 2, piece % 2

    def gifts(job, i):
        if job == 0:
            cols, to, half = slice_of(i)
        else:
            cols, to, half = pl.ds(0, HALF), 0, core
        there = job_cols(job)
        return (
            rcopy(bp.at[:, cols], bg.at[rows(z * TOK, TOK), there], jsend.at[i, 0], jrecv.at[job, 0], (to, me, half)),
            rcopy(cg.at[:, cols], gin.at[pl.ds(0, TOK), there], jsend.at[i, 1], jrecv.at[job, 1], (to, me, half)),
            rcopy(cw.at[:, cols], cwin.at[:, there], jsend.at[i, 2], jrecv.at[job, 2], (to, me, half)),
            rcopy(
                cg.at[pl.ds(0, 16), cols], gin.at[pl.ds(TOK, 16), there], jsend.at[i, 3], jrecv.at[job, 3],
                (to, me - 1, half),
            ),
        )

    def gifts_here():
        cols, there = pl.ds(CHUNK, CHUNK), job_cols(0)
        return (
            pltpu.make_async_copy(bp.at[:, cols], bg.at[rows(z * TOK, TOK), there], jrecv.at[0, 0]),
            pltpu.make_async_copy(cg.at[:, cols], gin.at[pl.ds(0, TOK), there], jrecv.at[0, 1]),
            pltpu.make_async_copy(cw.at[:, cols], cwin.at[:, there], jrecv.at[0, 2]),
        )

    def share(act, local):
        def some(copies, kinds):
            for kind in kinds:
                act(copies[kind])

        for job in (1, 2):
            @pl.when(sec == JOBS[job][0])
            def _():
                some(gifts(job, 0), (0, 1, 2))

                @pl.when(has_prev)
                def _():
                    some(gifts(job, 0), (3,))

        @pl.when(sec == 2)
        def _():
            for i in range(SPREAD):
                if i == 1:
                    @pl.when(core == 0)
                    def _():
                        some(gifts(0, 1), (0, 1, 2))

                    if local:
                        @pl.when(core == 1)
                        def _():
                            for copy in gifts_here():
                                copy.start()
                else:
                    some(gifts(0, i), (0, 1, 2))

                @pl.when(has_prev)
                def _():
                    some(gifts(0, i), (3,))

    def conv(job):
        there, width = job_cols(job), JOBS[job][2]
        wait_in(gin.at[pl.ds(0, TOK), there], jrecv.at[job, 1])
        wait_in(cwin.at[:, there], jrecv.at[job, 2])

        @pl.when(has_next)
        def _():
            wait_in(gin.at[pl.ds(TOK, 16), there], jrecv.at[job, 3])
            gext[pl.ds(TOK, 8), pl.ds(0, width)] = gin[pl.ds(TOK, 16), there].astype(F32)[0:8]

        @pl.when(jnp.logical_not(has_next))
        def _():
            gext[pl.ds(TOK, 8), pl.ds(0, width)] = jnp.zeros((8, width), F32)

        gext[pl.ds(0, TOK), pl.ds(0, width)] = gin[pl.ds(0, TOK), there].astype(F32)

        @pl.loop(0, width // 128)
        def _(i):
            lanes = pl.ds(pl.multiple_of(i * 128, 128), 128)
            cols = pl.ds(pl.multiple_of(JOBS[job][1] + i * 128, 128), 128)
            total = jnp.zeros((TOK, 128), F32)
            for tap in range(4):
                total = total + cwin[tap : tap + 1, cols] * gext[pl.ds(3 - tap, TOK), lanes]
            ag[rows(y * TOK, TOK), cols] = total.astype(BF16)

        for dy in range(1, NY):
            a_copy(job, dy).start()

    def a_copy(job, dy):
        block = ag.at[rows(y * TOK, TOK), job_cols(job)]
        return rcopy(block, block, asend.at[job, dy - 1], arecv.at[job, y], ydev(dy))

    place = (NSEC - 1 - sec) * 2 + core

    def product(job, shard):
        col, width = JOBS[job][1], JOBS[job][2]
        tall = rows(shard * TOK, TOK)
        psend[job, shard] = dot_nt(ag[:, pl.ds(col, width)], bg[tall, pl.ds(col, width)]).astype(BF16)

    def proj_back(job, shard, dy):
        to = (y + dy) % NY
        half = shard // 4
        which = place if job == 0 else core
        return rcopy(
            psend.at[job, shard, rows(to * TOK, TOK)],
            prec.at[which, y, :, rows((shard % 4) * TOK, TOK)],
            qsend.at[job, shard, 0 if dy == 0 else 1], qrecv.at[which, y],
            (JOBS[job][0], z * NY + to, half),
        )

    def proj_local(job, shard):
        return (sec == 2) & (shard // 4 == core) if job == 0 else sec == NSEC

    def proj_go(job, shard):
        product(job, shard)
        for dy in range(1, NY):
            proj_back(job, shard, dy).start()
        if job == 0:
            here = proj_local(job, shard)

            @pl.when(here)
            def _():
                prec[place, y, :, rows((shard % 4) * TOK, TOK)] = psend[job, shard, rows(y * TOK, TOK), :]

            @pl.when(jnp.logical_not(here))
            def _():
                proj_back(job, shard, 0).start()
        else:
            proj_back(job, shard, 0).start()

    def proj_sent(job):
        def one(shard, carry):
            wait_out(psend.at[job, shard, pl.ds(0, 3 * TOK)], qsend.at[job, shard, 1])
            if job == 0:
                @pl.when(jnp.logical_not(proj_local(job, shard)))
                def _():
                    proj_back(job, shard, 0).wait_send()
            else:
                proj_back(job, shard, 0).wait_send()
            return carry

        lax.fori_loop(0, NZ, one, 0)

    def proj_step(job, step):
        def one(i, carry):
            shard = (z - step + NZ) % NZ + i * ((z + step) % NZ - (z - step + NZ) % NZ)
            proj_go(job, shard)
            return carry

        lax.fori_loop(0, 1 if step in (0, 4) else 2, one, 0)

    def tokens_arrived(job):
        for dy in range(1, NY):
            i = (y + dy) % NY
            wait_in(ag.at[rows(i * TOK, TOK), job_cols(job)], arecv.at[job, i])

    own_down = pltpu.make_async_copy(down, wdn.at[core], lsem.at[1])
    own_up = pltpu.make_async_copy(up, wup.at[core], lsem.at[2])
    own_pre = pltpu.make_async_copy(pre.at[rows(core * 256, 256)], prev_.at[core], lsem.at[3])
    give_down = rcopy(down, wdn.at[core], wsend.at[0], wrecv.at[0], partner)
    give_up = rcopy(up, wup.at[core], wsend.at[1], wrecv.at[1], partner)
    give_pre = rcopy(pre.at[rows(other * 256, 256)], prev_.at[core], wsend.at[2], wrecv.at[2], partner)
    def block_copy(e):
        return rcopy(
            sbuf.at[rows(e * CAP, CAP)],
            xin.at[core, rows((me % 16) * CAP, CAP)],
            xsend.at[e], xrecv.at[me % 16, core], (sec, e, mine),
        )

    def block_local(e):
        return pltpu.make_async_copy(
            sbuf.at[rows(e * CAP, CAP)],
            xin.at[core, rows((me % 16) * CAP, CAP)],
            xrecv.at[me % 16, core],
        )

    @pl.when(active)
    def _():
        own_down.start()
        own_up.start()
        own_pre.start()

        line = lax.broadcasted_iota(jnp.int32, (NEXP * CAP, TOK), 0)
        expert = line // CAP
        rank = line % CAP
        first = ids[0:1, :] == expert
        second = ids[1:2, :] == expert
        named = first | second
        gates = codes[...].astype(F32) / 256.0
        gate = jnp.where(first, gates[0:1, :], 0.0) + jnp.where(second, gates[1:2, :], 0.0)
        low = lax.broadcasted_iota(jnp.int32, (TOK, TOK), 0) < lax.broadcasted_iota(jnp.int32, (TOK, TOK), 1)
        before = jnp.dot(
            jnp.where(named, 1.0, 0.0).astype(BF16),
            jnp.where(low, 1.0, 0.0).astype(BF16),
            preferred_element_type=F32,
        )
        here = named & (before == rank.astype(F32))
        placed = jnp.where(here, gate, 0.0).astype(BF16)
        for tile in range(4):
            cols = pl.ds(tile * 512, 512)
            sbuf[:, cols] = jnp.dot(placed, og[:, cols], preferred_element_type=F32).astype(BF16)
        comb[...] = jnp.where(here, 1.0, 0.0).T.astype(BF16)

    pl.semaphore_wait(barrier, 2 * NEXP - 1 + 24 + 6 * has_prev.astype(jnp.int32) + 6 * has_next.astype(jnp.int32))

    @pl.when(has_next)
    def _():
        halo_i_out.start()

    share(lambda copy: copy.start(), True)

    def dispatch(first_turn, turns):
        def send_block(i, carry):
            turn = i // 8
            zt = (z - turn + 8) % 4 + 4 * ((i // 4) % 2)
            e = zt * NY + (y + i) % NY
            own = (e == me) & (mine == core)

            @pl.when(own)
            def _():
                block_local(e).start()

            @pl.when(jnp.logical_not(own))
            def _():
                block_copy(e).start()

            return carry

        lax.fori_loop(first_turn * 8, (first_turn + turns) * 8, send_block, 0)

    both = active & runs

    @pl.when(both)
    def _():
        ring_go(0, 1)
        dispatch(0, 1)

    @pl.when(active & jnp.logical_not(runs))
    def _():
        dispatch(0, 4)

    @pl.when(active)
    def _():
        give_down.start()
        give_pre.start()
        give_up.start()

    @pl.when(jnp.logical_not(active))
    def _():
        ring_go(1, 1)
        ring_go(2, 1)

    @pl.when(has_prev)
    def _():
        wait_in(halo_i, hrecv.at[1])

    @pl.when(jnp.logical_not(has_prev))
    def _():
        halo_i[...] = jnp.zeros_like(halo_i)

    iext[pl.ds(0, 8), :] = halo_i[...].astype(F32)[8:16]
    iext[pl.ds(8, TOK), :] = ci[...].astype(F32)
    tap_p[...] = jnp.zeros_like(tap_p)

    for quarter in range(4):
        @pl.loop(0, 4)
        def _(i):
            cols = pl.ds(pl.multiple_of(quarter * 512 + i * 128, 128), 128)
            lanes = pl.ds(pl.multiple_of(i * 128, 128), 128)
            grad = cg[:, cols].astype(F32)
            for tap in range(4):
                term = grad * iext[pl.ds(5 + tap, TOK), cols]
                tap_p[quarter, tap : tap + 1, lanes] = jnp.sum(term, axis=0, keepdims=True)

    def tap_scatter(dy):
        to = (y + dy) % NY
        return rcopy(tap_p.at[to], tap_r.at[y], tsend.at[0, dy - 1], trecv.at[0, y], ydev(dy))

    for dy in range(1, NY):
        tap_scatter(dy).start()

    @pl.when(runs)
    def _():
        conv(0)

    @pl.when(jnp.logical_not(active))
    def _():
        conv(1)
        conv(2)
        for job in (1, 2):
            ring_go(job, 2)

    @pl.when(both)
    def _():
        ring_go(0, 2)
        dispatch(1, 1)
        ring_go(0, 3)
        dispatch(2, 1)

    tap_r[y] = tap_p[y]
    for dy in range(1, NY):
        wait_in(tap_r.at[(y + dy) % NY], trecv.at[0, (y + dy) % NY])
    tap_s[...] = (tap_r[0] + tap_r[1]) + (tap_r[2] + tap_r[3])

    def tap_gather(dz):
        return rcopy(tap_s, tap_z.at[z], tsend.at[1, dz - 1], trecv.at[1, z], zdev(dz))

    for dz in range(1, NZ):
        tap_gather(dz).start()

    def back(src, half):
        return rcopy(
            yout.at[half, rows(src * CAP, CAP)],
            ret.at[rows(me * CAP, CAP)],
            ysend.at[src, half], yrecv.at[me],
            (sec, core * 16 + src, half),
        )

    def back_local(src):
        return pltpu.make_async_copy(
            yout.at[core, rows(src * CAP, CAP)], ret.at[rows(me * CAP, CAP)], yrecv.at[me]
        )

    def expert_chunk(turn):
        zs = (turn + z) % 4
        block = rows(zs * 64, 64)

        def arrive(i, carry):
            src = zs * NY + i // 2
            wait_in(xin.at[i % 2, rows(src * CAP, CAP)], xrecv.at[src, i % 2])
            return carry

        lax.fori_loop(0, 8, arrive, 0)
        if turn == 0:
            own_down.wait()
            wait_in(wdn.at[other], wrecv.at[0])
            own_pre.wait()
            wait_in(prev_.at[other], wrecv.at[2])
        x0 = xin[0, block, :]
        x1 = xin[1, block, :]
        grads = []
        for h in range(2):
            hidden = dot_nt(x0, wdn[h, :, 0:HALF]) + dot_nt(x1, wdn[h, :, HALF:])
            slope = silu_slope(prev_[h, block, :].astype(F32))
            grads.append((hidden * slope).astype(BF16))
        if turn == 0:
            own_up.wait()
            wait_in(wup.at[other], wrecv.at[1])
        for half in range(2):
            @pl.loop(0, 4)
            def _(t):
                wide = pl.ds(pl.multiple_of(half * HALF + t * 512, 512), 512)
                cols = pl.ds(pl.multiple_of(t * 512, 512), 512)
                value = dot_nt(grads[0], wup[0, wide, :]) + dot_nt(grads[1], wup[1, wide, :])
                yout[half, block, cols] = value.astype(BF16)

        def give(i, carry):
            src = zs * NY + (y + i // 2) % NY
            own = (core * 16 + src == me) & (i % 2 == core)

            @pl.when(own)
            def _():
                back_local(src).start()

            @pl.when(jnp.logical_not(own))
            def _():
                back(src, i % 2).start()

            return carry

        lax.fori_loop(0, 8, give, 0)

    @pl.when(active)
    def _():
        expert_chunk(0)

        @pl.when(runs)
        def _():
            ring_go(0, 4)
            dispatch(3, 1)

        expert_chunk(1)
        expert_chunk(2)

        @pl.when(runs)
        def _():
            tokens_arrived(0)
            for step in range(4):
                proj_step(0, step)
            ring_arrived(0, 4)
            proj_step(0, 4)

    @pl.when(jnp.logical_not(active))
    def _():
        for job in (1, 2):
            ring_go(job, 3)
        for job in (1, 2):
            tokens_arrived(job)
            proj_step(job, 0)
            proj_step(job, 1)
        for job in (1, 2):
            ring_go(job, 4)
        for job in (1, 2):
            proj_step(job, 2)
            proj_step(job, 3)
        for job in (1, 2):
            ring_arrived(job, 4)
            proj_step(job, 4)

    tap_z[z] = tap_s[...]
    for dz in range(1, NZ):
        wait_in(tap_z.at[(z + dz) % NZ], trecv.at[1, (z + dz) % NZ])
    total = tap_z[0]
    for i in range(1, NZ):
        total = total + tap_z[i]
    tap_t[...] = total

    def tap_share(dy):
        return rcopy(tap_t, tap_o.at[y], tsend.at[2, dy - 1], trecv.at[2, y], ydev(dy))

    for dy in range(1, NY):
        tap_share(dy).start()

    def result_out(tile):
        cols = pl.ds(tile * 512, 512)
        return rcopy(res.at[:, cols], out.at[:, cols], osend.at[tile], orecv.at[tile], (sec - 1, me, core))

    @pl.when(active)
    def _():
        expert_chunk(3)

    @pl.when(active)
    def _():
        def partial(which, carry):
            for i in range(NY):
                own = (sec == 2) & (which == place) & (i == y)

                @pl.when(jnp.logical_not(own))
                def _():
                    wait_in(prec.at[which, i], qrecv.at[which, i])

            for i in range(NY):
                for tile in range(4):
                    cols = pl.ds((tile * NY + i) * TOK, TOK)
                    base[:, cols] += prec[which, i, :, pl.ds(tile * TOK, TOK)].astype(F32)
            return carry

        base[...] = og[...].astype(F32)
        lax.fori_loop(0, jnp.where(sec == 2, 2 * SPREAD, 2), partial, 0)

        def arrive(i, carry):
            wait_in(ret.at[rows(i * CAP, CAP)], yrecv.at[i])
            return carry

        lax.fori_loop(0, NEXP, arrive, 0)
        for tile in range(4):
            cols = pl.ds(tile * 512, 512)
            moe = jnp.dot(comb[...], ret[:, cols], preferred_element_type=F32)
            res[:, cols] = (base[:, cols] + moe).astype(BF16)
            result_out(tile).start()

    @pl.when(fed)
    def _():
        for tile in range(4):
            wait_in(out.at[:, pl.ds(tile * 512, 512)], orecv.at[tile])

    @pl.when(jnp.logical_not(fed))
    def _():
        out[...] = jnp.zeros_like(out)

    tap_o[y] = tap_t[...]
    for dy in range(1, NY):
        wait_in(tap_o.at[(y + dy) % NY], trecv.at[2, (y + dy) % NY])
    for quarter in range(4):
        kout[:, pl.ds(quarter * 512, 512)] = tap_o[quarter, 0:4, :]

    share(lambda copy: copy.wait_send(), False)

    def ring_sent(job):
        for step in range(1, 5):
            ring(job, step, True).wait_send()
            ring(job, step, False).wait_send()
        for dy in range(1, NY):
            a_copy(job, dy).wait_send()
        proj_sent(job)

    @pl.when(runs)
    def _():
        ring_sent(0)

    @pl.when(jnp.logical_not(active))
    def _():
        ring_sent(1)
        ring_sent(2)

    @pl.when(has_next)
    def _():
        halo_i_out.wait_send()

    for dy in range(1, NY):
        tap_scatter(dy).wait_send()
        tap_share(dy).wait_send()
    for dz in range(1, NZ):
        tap_gather(dz).wait_send()

    @pl.when(active)
    def _():
        give_down.wait_send()
        give_up.wait_send()
        give_pre.wait_send()
        for tile in range(4):
            result_out(tile).wait_send()

        def sent(e, carry):
            own = (e == me) & (mine == core)

            @pl.when(jnp.logical_not(own))
            def _():
                block_copy(e).wait_send()

            mirror = (core * 16 + e // 2 == me) & (e % 2 == core)

            @pl.when(jnp.logical_not(mirror))
            def _():
                back(e // 2, e % 2).wait_send()

            return carry

        lax.fori_loop(0, NEXP, sent, 0)


def shards(
    out_grad, expert_ids, gate_codes, up_weight, down_weight, pre_act, conv_grad, conv_input, conv_weight, in_proj
):
    vmem = pl.BlockSpec(memory_space=pltpu.VMEM)
    anywhere = pl.BlockSpec(memory_space=pl.ANY)
    dma = pltpu.SemaphoreType.DMA
    out, kout = pl.pallas_call(
        kernel,
        out_shape=(
            jax.ShapeDtypeStruct((TOK, HALF), BF16),
            jax.ShapeDtypeStruct((4, HALF), F32),
        ),
        in_specs=[vmem] * 7 + [anywhere] * 3,
        out_specs=(vmem, vmem),
        scratch_shapes=[
            pltpu.VMEM((2, 512, 4096), BF16),
            pltpu.VMEM((2, 4096, 512), BF16),
            pltpu.VMEM((2, 256, 512), BF16),
            pltpu.VMEM((512, HALF), BF16),
            pltpu.VMEM((2, 256, HALF), BF16),
            pltpu.VMEM((2, 256, HALF), BF16),
            pltpu.VMEM((512, HALF), BF16),
            pltpu.VMEM((TOK, 512), BF16),
            pltpu.VMEM((TOK, HALF), BF16),
            pltpu.VMEM((NZ * TOK, WIDE), BF16),
            pltpu.VMEM((NY * TOK, WIDE), BF16),
            pltpu.VMEM((TOK + 16, WIDE), BF16),
            pltpu.VMEM((4, WIDE), F32),
            pltpu.VMEM((16, HALF), BF16),
            pltpu.VMEM((TOK + 8, HALF), F32),
            pltpu.VMEM((TOK + 8, HALF), F32),
            pltpu.VMEM((3, NZ, NY * TOK, TOK), BF16),
            pltpu.VMEM((2 * SPREAD, NY, TOK, 512), BF16),
            pltpu.VMEM((TOK, HALF), F32),
            pltpu.VMEM((NY, 8, 512), F32),
            pltpu.VMEM((NY, 8, 512), F32),
            pltpu.VMEM((8, 512), F32),
            pltpu.VMEM((NZ, 8, 512), F32),
            pltpu.VMEM((8, 512), F32),
            pltpu.VMEM((NY, 8, 512), F32),
            dma((5,)),
            dma((3,)), dma((3,)),
            dma((2,)), dma((2,)),
            dma((4,)), dma((4,)),
            dma((3, 4, 2)), dma((3, 4, 2)),
            dma((NEXP,)), dma((16, 2)),
            dma((16, 2)), dma((NEXP,)),
            dma((3, 3)), dma((3, NY)),
            dma((SPREAD, 4)), dma((3, 4)),
            dma((3, NZ, 2)), dma((2 * SPREAD, NY)),
            dma((3, 7)), dma((3, NZ)),
        ],
        compiler_params=pltpu.CompilerParams(has_side_effects=True, collective_id=0, vmem_limit_bytes=63 * 1024 * 1024),
        name="layer_backward",
    )(
        out_grad[0], expert_ids[0].T, gate_codes[0].T, conv_grad[0], conv_input[0], conv_weight[0], in_proj[0],
        up_weight[0, 0], down_weight[0, 0], pre_act[0, 0],
    )
    return out[None], kout[None]


def solution(mesh):
    in_specs = (
        P("section", "expert", "mp"),
        P("section", "expert", None),
        P("section", "expert", None),
        P("section", "expert", None, "mp"),
        P("section", "expert", "mp", None),
        P("section", "expert", None, "mp"),
        P("section", "expert", "mp"),
        P("section", "expert", "mp"),
        P("section", None, "mp"),
        P("section", "expert", "mp"),
    )
    out_specs = (P("section", "expert", "mp"), P("section", None, "mp"))
    return jax.shard_map(shards, mesh=mesh, in_specs=in_specs, out_specs=out_specs, check_vma=False)
```

time: 183 us -> 162 us (0.89)
  the two profiles are of different devices: /device:TPU:37 before, /device:TPU:133 now
where the time goes in v2:
time: 162 us
  Pallas kernels  158 us (98%)
  local copies, waits for them, and re-layouts  3.26 us (2%)
    pallas_call x1, Pallas kernels, shards(): pl.pallas_call(kernel, out_shape=(jax.ShapeDtypeStruct((TOK, HALF), BF16)...  158 us
    unnamed x2, local copies, waits for them, and re-layouts  3.26 us

profile of v2, /device:TPU:133, one launch (start us, length us, event | category | flops | bytes accessed | tf_op | source)
XLA Modules:
  0.0 162.0 jit_solution(3158404445605296962)
XLA Ops:
  0.6 158.1 %layer_backward.1 = (bf16[128,2048]{1,0:T(8,128)(2,1)}, f32[4,2048]{1,0:T(4,128)}) custom-call(bf16[128,2048]{1,0:T(8,128)(2,1)} %bitcast.18, s32[2,128]{1,0:T(2,128)} %bitcast.26, s32[2,128]{1,0:T(2,128)} %bitcast.27, bf16[128,2048]{1,0:T(8,128)(2,1)} %bitcast.19, bf16[128,2048]{1,0:T(8,128)(2,1)} %bitcast.20, f32[4,2048]{1,0:T(4,128)} %bitcast.24, ...), custom_call_target="tpu_custom_call" | custom-call | tf_op jit(solution)/shard_map/layer_backward/pallas_call | solution.py:679
  158.7 1.9 %copy.14 = bf16[1,128,2048]{2,1,0:T(8,128)(2,1)} copy(bf16[1,128,2048]{2,1,0:T(8,128)(2,1)} %bitcast.23) | data formatting | bytes 1048576
  160.6 1.4 copy.15

commit v3 on v2

--- a/solution.py
+++ b/solution.py
@@ -34,12 +34,12 @@
 def kernel(
     og, ids, codes, cg, ci, cw, bp, up, down, pre,
     out, kout,
-    wdn, wup, prev_, sbuf, xin, yout, ret, comb, res,
-    bg, ag, gin, cwin, halo_i, gext, iext, psend, prec, base,
+    wdn, wup, prev_, sbuf, xin, yout, ret, comb, combt, res, part_in, ret_late, comb_late,
+    bg, ag, gin, cwin, halo_i, gext, iext, psend, pin, prec, base,
     tap_p, tap_r, tap_s, tap_z, tap_t, tap_o,
     lsem, wsend, wrecv, hsend, hrecv, osend, orecv,
     bsend, brecv, xsend, xrecv, ysend, yrecv, asend, arecv,
-    jsend, jrecv, qsend, qrecv, tsend, trecv,
+    jsend, jrecv, lsend, lrecv, csend, crecv, esend, erecv, qsend, qrecv, tsend, trecv,
 ):
     sec = lax.axis_index("section")
     me = lax.axis_index("expert")
@@ -231,64 +231,67 @@
         block = ag.at[rows(y * TOK, TOK), job_cols(job)]
         return rcopy(block, block, asend.at[job, dy - 1], arecv.at[job, y], ydev(dy))
 
-    place = (NSEC - 1 - sec) * 2 + core
-
-    def product(job, shard):
-        col, width = JOBS[job][1], JOBS[job][2]
-        tall = rows(shard * TOK, TOK)
-        psend[job, shard] = dot_nt(ag[:, pl.ds(col, width)], bg[tall, pl.ds(col, width)]).astype(BF16)
+    place = NSEC - 1 - sec
+
+    def halves(job, shard):
+        return rcopy(
+            psend.at[job, shard], pin.at[job, shard % 4], esend.at[job, shard % 4], erecv.at[job, shard % 4], partner
+        )
 
     def proj_back(job, shard, dy):
         to = (y + dy) % NY
-        half = shard // 4
-        which = place if job == 0 else core
         return rcopy(
             psend.at[job, shard, rows(to * TOK, TOK)],
-            prec.at[which, y, :, rows((shard % 4) * TOK, TOK)],
-            qsend.at[job, shard, 0 if dy == 0 else 1], qrecv.at[which, y],
-            (JOBS[job][0], z * NY + to, half),
-        )
-
-    def proj_local(job, shard):
-        return (sec == 2) & (shard // 4 == core) if job == 0 else sec == NSEC
-
-    def proj_go(job, shard):
-        product(job, shard)
-        for dy in range(1, NY):
-            proj_back(job, shard, dy).start()
-        if job == 0:
-            here = proj_local(job, shard)
-
-            @pl.when(here)
-            def _():
-                prec[place, y, :, rows((shard % 4) * TOK, TOK)] = psend[job, shard, rows(y * TOK, TOK), :]
-
-            @pl.when(jnp.logical_not(here))
-            def _():
-                proj_back(job, shard, 0).start()
-        else:
-            proj_back(job, shard, 0).start()
-
-    def proj_sent(job):
-        def one(shard, carry):
-            wait_out(psend.at[job, shard, pl.ds(0, 3 * TOK)], qsend.at[job, shard, 1])
-            if job == 0:
-                @pl.when(jnp.logical_not(proj_local(job, shard)))
-                def _():
-                    proj_back(job, shard, 0).wait_send()
-            else:
-                proj_back(job, shard, 0).wait_send()
-            return carry
-
-        lax.fori_loop(0, NZ, one, 0)
+            prec.at[place if job == 0 else 0, y, :, rows((shard % 4) * TOK, TOK)],
+            qsend.at[job, shard % 4, 0 if dy == 0 else 1], qrecv.at[place if job == 0 else 0, y],
+            (JOBS[job][0] - 1, z * NY + to, core),
+        )
 
     def proj_step(job, step):
+        col, width = JOBS[job][1], JOBS[job][2]
+
         def one(i, carry):
             shard = (z - step + NZ) % NZ + i * ((z + step) % NZ - (z - step + NZ) % NZ)
-            proj_go(job, shard)
+            tall = rows(shard * TOK, TOK)
+            psend[job, shard] = dot_nt(ag[:, pl.ds(col, width)], bg[tall, pl.ds(col, width)]).astype(BF16)
+
+            @pl.when(shard // 4 != core)
+            def _():
+                halves(job, shard).start()
+
             return carry
 
         lax.fori_loop(0, 1 if step in (0, 4) else 2, one, 0)
+
+    def proj_finish(job, step):
+        def one(i, carry):
+            shard = (z - step + NZ) % NZ + i * ((z + step) % NZ - (z - step + NZ) % NZ)
+
+            @pl.when(shard // 4 == core)
+            def _():
+                wait_in(pin.at[job, shard % 4], erecv.at[job, shard % 4])
+                psend[job, shard] = (psend[job, shard].astype(F32) + pin[job, shard % 4].astype(F32)).astype(BF16)
+                for dy in range(1, NY):
+                    proj_back(job, shard, dy).start()
+                if job == 1:
+                    prec[0, y, :, rows((shard % 4) * TOK, TOK)] = psend[job, shard, rows(y * TOK, TOK), :]
+                else:
+                    proj_back(job, shard, 0).start()
+
+            return carry
+
+        lax.fori_loop(0, 1 if step in (0, 4) else 2, one, 0)
+
+    def proj_sent(job):
+        def one(i, carry):
+            shard = core * 4 + i
+            wait_out(psend.at[job, shard, pl.ds(0, 3 * TOK)], qsend.at[job, i, 1])
+            if job != 1:
+                proj_back(job, shard, 0).wait_send()
+            halves(job, other * 4 + i).wait_send()
+            return carry
+
+        lax.fori_loop(0, 4, one, 0)
 
     def tokens_arrived(job):
         for dy in range(1, NY):
@@ -301,6 +304,15 @@
     give_down = rcopy(down, wdn.at[core], wsend.at[0], wrecv.at[0], partner)
     give_up = rcopy(up, wup.at[core], wsend.at[1], wrecv.at[1], partner)
     give_pre = rcopy(pre.at[rows(other * 256, 256)], prev_.at[core], wsend.at[2], wrecv.at[2], partner)
+    def late(i):
+        return (z + 1) % 4 + 4 * i
+
+    def give_late(i):
+        return rcopy(
+            combt.at[rows(late(i) * 64, 64)], comb_late.at[pl.ds(i * 64, 64)], csend.at[i], crecv.at[i],
+            (sec - 1, me, core),
+        )
+
     def block_copy(e):
         return rcopy(
             sbuf.at[rows(e * CAP, CAP)],
@@ -340,7 +352,11 @@
         for tile in range(4):
             cols = pl.ds(tile * 512, 512)
             sbuf[:, cols] = jnp.dot(placed, og[:, cols], preferred_element_type=F32).astype(BF16)
-        comb[...] = jnp.where(here, 1.0, 0.0).T.astype(BF16)
+        ones = jnp.where(here, 1.0, 0.0)
+        combt[...] = ones.astype(BF16)
+        comb[...] = ones.T.astype(BF16)
+        for i in range(2):
+            ret[rows(late(i) * 64, 64), :] = jnp.zeros((64, HALF), BF16)
 
     pl.semaphore_wait(barrier, 2 * NEXP - 1 + 24 + 6 * has_prev.astype(jnp.int32) + 6 * has_next.astype(jnp.int32))
 
@@ -385,6 +401,8 @@
         give_down.start()
         give_pre.start()
         give_up.start()
+        for i in range(2):
+            give_late(i).start()
 
     @pl.when(jnp.logical_not(active))
     def _():
@@ -455,6 +473,14 @@
             ret.at[rows(me * CAP, CAP)],
             ysend.at[src, half], yrecv.at[me],
             (sec, core * 16 + src, half),
+        )
+
+    def back_late(src, half):
+        return rcopy(
+            yout.at[half, rows(src * CAP, CAP)],
+            ret_late.at[rows(((z // 4) * NY + y) * CAP, CAP)],
+            lsend.at[src % NY, half], lrecv.at[(z // 4) * NY + y],
+            (sec - 1, core * 16 + src, half),
         )
 
     def back_local(src):
@@ -497,6 +523,9 @@
 
         def give(i, carry):
             src = zs * NY + (y + i // 2) % NY
+            if turn == 3:
+                back_late(src, i % 2).start()
+                return carry
             own = (core * 16 + src == me) & (i % 2 == core)
 
             @pl.when(own)
@@ -513,23 +542,31 @@
 
     @pl.when(active)
     def _():
-        expert_chunk(0)
-
         @pl.when(runs)
         def _():
             ring_go(0, 4)
             dispatch(3, 1)
 
-        expert_chunk(1)
-        expert_chunk(2)
+        expert_chunk(0)
 
         @pl.when(runs)
         def _():
             tokens_arrived(0)
             for step in range(4):
                 proj_step(0, step)
+            for step in range(4):
+                proj_finish(0, step)
+
+        expert_chunk(1)
+
+        @pl.when(runs)
+        def _():
             ring_arrived(0, 4)
             proj_step(0, 4)
+            proj_finish(0, 4)
+
+        expert_chunk(2)
+
 
     @pl.when(jnp.logical_not(active))
     def _():
@@ -539,14 +576,20 @@
             tokens_arrived(job)
             proj_step(job, 0)
             proj_step(job, 1)
+            proj_finish(job, 0)
+            proj_finish(job, 1)
         for job in (1, 2):
             ring_go(job, 4)
         for job in (1, 2):
             proj_step(job, 2)
             proj_step(job, 3)
+            proj_finish(job, 2)
+            proj_finish(job, 3)
         for job in (1, 2):
             ring_arrived(job, 4)
             proj_step(job, 4)
+        for job in (1, 2):
+            proj_finish(job, 4)
 
     tap_z[z] = tap_s[...]
     for dz in range(1, NZ):
@@ -564,17 +607,33 @@
 
     def result_out(tile):
         cols = pl.ds(tile * 512, 512)
-        return rcopy(res.at[:, cols], out.at[:, cols], osend.at[tile], orecv.at[tile], (sec - 1, me, core))
+        return rcopy(res.at[:, cols], part_in.at[:, cols], osend.at[tile], orecv.at[tile], (sec - 1, me, core))
 
     @pl.when(active)
     def _():
         expert_chunk(3)
 
     @pl.when(active)
+    def _():
+        def arrive(i, carry):
+            @pl.when((i // NY) % 4 != (z + 1) % 4)
+            def _():
+                wait_in(ret.at[rows(i * CAP, CAP)], yrecv.at[i])
+
+            return carry
+
+        lax.fori_loop(0, NEXP, arrive, 0)
+        for tile in range(4):
+            cols = pl.ds(tile * 512, 512)
+            moe = jnp.dot(comb[...], ret[:, cols], preferred_element_type=F32)
+            res[:, cols] = (og[:, cols].astype(F32) + moe).astype(BF16)
+            result_out(tile).start()
+
+    @pl.when(fed)
     def _():
         def partial(which, carry):
             for i in range(NY):
-                own = (sec == 2) & (which == place) & (i == y)
+                own = (sec == 0) & (i == y)
 
                 @pl.when(jnp.logical_not(own))
                 def _():
@@ -586,24 +645,23 @@
                     base[:, cols] += prec[which, i, :, pl.ds(tile * TOK, TOK)].astype(F32)
             return carry
 
-        base[...] = og[...].astype(F32)
-        lax.fori_loop(0, jnp.where(sec == 2, 2 * SPREAD, 2), partial, 0)
+        base[...] = jnp.zeros_like(base)
+        lax.fori_loop(0, jnp.where(sec == 1, SPREAD, 1), partial, 0)
+        for i in range(2):
+            wait_in(comb_late.at[pl.ds(i * 64, 64)], crecv.at[i])
+        last = comb_late[...].astype(F32).T.astype(BF16)
+        for tile in range(4):
+            wait_in(part_in.at[:, pl.ds(tile * 512, 512)], orecv.at[tile])
 
         def arrive(i, carry):
-            wait_in(ret.at[rows(i * CAP, CAP)], yrecv.at[i])
-            return carry
-
-        lax.fori_loop(0, NEXP, arrive, 0)
+            wait_in(ret_late.at[rows(i * CAP, CAP)], lrecv.at[i])
+            return carry
+
+        lax.fori_loop(0, 8, arrive, 0)
         for tile in range(4):
             cols = pl.ds(tile * 512, 512)
-            moe = jnp.dot(comb[...], ret[:, cols], preferred_element_type=F32)
-            res[:, cols] = (base[:, cols] + moe).astype(BF16)
-            result_out(tile).start()
-
-    @pl.when(fed)
-    def _():
-        for tile in range(4):
-            wait_in(out.at[:, pl.ds(tile * 512, 512)], orecv.at[tile])
+            moe = jnp.dot(last, ret_late[:, cols], preferred_element_type=F32)
+            out[:, cols] = (base[:, cols] + part_in[:, cols].astype(F32) + moe).astype(BF16)
 
     @pl.when(jnp.logical_not(fed))
     def _():
@@ -649,6 +707,8 @@
         give_down.wait_send()
         give_up.wait_send()
         give_pre.wait_send()
+        for i in range(2):
+            give_late(i).wait_send()
         for tile in range(4):
             result_out(tile).wait_send()
 
@@ -660,10 +720,15 @@
                 block_copy(e).wait_send()
 
             mirror = (core * 16 + e // 2 == me) & (e % 2 == core)
-
-            @pl.when(jnp.logical_not(mirror))
+            final = (e // 8) % 4 == (z + 3) % 4
+
+            @pl.when(jnp.logical_not(mirror | final))
             def _():
                 back(e // 2, e % 2).wait_send()
+
+            @pl.when(final)
+            def _():
+                back_late(e // 2, e % 2).wait_send()
 
             return carry
 
@@ -693,7 +758,11 @@
             pltpu.VMEM((2, 256, HALF), BF16),
             pltpu.VMEM((512, HALF), BF16),
             pltpu.VMEM((TOK, 512), BF16),
+            pltpu.VMEM((512, TOK), BF16),
             pltpu.VMEM((TOK, HALF), BF16),
+            pltpu.VMEM((TOK, HALF), BF16),
+            pltpu.VMEM((TOK, HALF), BF16),
+            pltpu.VMEM((TOK, TOK), BF16),
             pltpu.VMEM((NZ * TOK, WIDE), BF16),
             pltpu.VMEM((NY * TOK, WIDE), BF16),
             pltpu.VMEM((TOK + 16, WIDE), BF16),
@@ -702,7 +771,8 @@
             pltpu.VMEM((TOK + 8, HALF), F32),
             pltpu.VMEM((TOK + 8, HALF), F32),
             pltpu.VMEM((3, NZ, NY * TOK, TOK), BF16),
-            pltpu.VMEM((2 * SPREAD, NY, TOK, 512), BF16),
+            pltpu.VMEM((3, 4, NY * TOK, TOK), BF16),
+            pltpu.VMEM((SPREAD, NY, TOK, 512), BF16),
             pltpu.VMEM((TOK, HALF), F32),
             pltpu.VMEM((NY, 8, 512), F32),
             pltpu.VMEM((NY, 8, 512), F32),
@@ -719,7 +789,10 @@
             dma((16, 2)), dma((NEXP,)),
             dma((3, 3)), dma((3, NY)),
             dma((SPREAD, 4)), dma((3, 4)),
-            dma((3, NZ, 2)), dma((2 * SPREAD, NY)),
+            dma((NY, 2)), dma((8,)),
+            dma((2,)), dma((2,)),
+            dma((3, 4)), dma((3, 4)),
+            dma((3, 4, 2)), dma((SPREAD, NY)),
             dma((3, 7)), dma((3, NZ)),
         ],
         compiler_params=pltpu.CompilerParams(has_side_effects=True, collective_id=0, vmem_limit_bytes=63 * 1024 * 1024),

time: 162 us -> 156 us (0.963)
  the two profiles are of different devices: /device:TPU:133 before, /device:TPU:37 now
where the time goes in v3:
time: 156 us
  Pallas kernels  152 us (97%)
  local copies, waits for them, and re-layouts  3.26 us (2%)
    pallas_call x1, Pallas kernels, shards(): pl.pallas_call(kernel, out_shape=(jax.ShapeDtypeStruct((TOK, HALF), BF16)...  152 us
    unnamed x2, local copies, waits for them, and re-layouts  3.26 us

profile of v3, /device:TPU:37, one launch (start us, length us, event | category | flops | bytes accessed | tf_op | source)
XLA Modules:
  0.0 156.1 jit_solution(8368212230277941240)
XLA Ops:
  0.6 152.2 %layer_backward.1 = (bf16[128,2048]{1,0:T(8,128)(2,1)}, f32[4,2048]{1,0:T(4,128)}) custom-call(bf16[128,2048]{1,0:T(8,128)(2,1)} %bitcast.18, s32[2,128]{1,0:T(2,128)} %bitcast.26, s32[2,128]{1,0:T(2,128)} %bitcast.27, bf16[128,2048]{1,0:T(8,128)(2,1)} %bitcast.19, bf16[128,2048]{1,0:T(8,128)(2,1)} %bitcast.20, f32[4,2048]{1,0:T(4,128)} %bitcast.24, ...), custom_call_target="tpu_custom_call" | custom-call | tf_op jit(solution)/shard_map/layer_backward/pallas_call | solution.py:744
  152.9 1.9 %copy.14 = bf16[1,128,2048]{2,1,0:T(8,128)(2,1)} copy(bf16[1,128,2048]{2,1,0:T(8,128)(2,1)} %bitcast.23) | data formatting | bytes 1048576
  154.8 1.4 copy.15

commit v4 on v3

--- a/solution.py
+++ b/solution.py
@@ -576,11 +576,11 @@
             tokens_arrived(job)
             proj_step(job, 0)
             proj_step(job, 1)
-            proj_finish(job, 0)
-            proj_finish(job, 1)
         for job in (1, 2):
             ring_go(job, 4)
         for job in (1, 2):
+            proj_finish(job, 0)
+            proj_finish(job, 1)
             proj_step(job, 2)
             proj_step(job, 3)
             proj_finish(job, 2)

time: 156 us -> 156 us (level)
  no operation moved by 1% of the time
where the time goes in v4:
time: 156 us
  Pallas kernels  152 us (97%)
  local copies, waits for them, and re-layouts  3.26 us (2%)
    pallas_call x1, Pallas kernels, shards(): pl.pallas_call(kernel, out_shape=(jax.ShapeDtypeStruct((TOK, HALF), BF16)...  152 us
    unnamed x2, local copies, waits for them, and re-layouts  3.26 us

profile of v4, /device:TPU:37, one launch (start us, length us, event | category | flops | bytes accessed | tf_op | source)
XLA Modules:
  0.0 156.1 jit_solution(14309649030929419337)
XLA Ops:
  0.6 152.2 %layer_backward.1 = (bf16[128,2048]{1,0:T(8,128)(2,1)}, f32[4,2048]{1,0:T(4,128)}) custom-call(bf16[128,2048]{1,0:T(8,128)(2,1)} %bitcast.18, s32[2,128]{1,0:T(2,128)} %bitcast.26, s32[2,128]{1,0:T(2,128)} %bitcast.27, bf16[128,2048]{1,0:T(8,128)(2,1)} %bitcast.19, bf16[128,2048]{1,0:T(8,128)(2,1)} %bitcast.20, f32[4,2048]{1,0:T(4,128)} %bitcast.24, ...), custom_call_target="tpu_custom_call" | custom-call | tf_op jit(solution)/shard_map/layer_backward/pallas_call | solution.py:744
  152.9 1.9 %copy.14 = bf16[1,128,2048]{2,1,0:T(8,128)(2,1)} copy(bf16[1,128,2048]{2,1,0:T(8,128)(2,1)} %bitcast.23) | data formatting | bytes 1048576
  154.8 1.4 copy.15
